TPU v7x, 32 devices: a whole 2x2x4 slice. The times are simulated.
32 devices in a mesh: prow: 4 (over y, x), pcol: 8 (over z, core).
Axes of the slice: x: 2, y: 2, z: 4, core: 2. Of those that a mesh axis runs over, the one named last changes fastest.
Arguments:
- anc_inverse: bfloat16 [6, 1024, 3, 2048], P(None, 'prow', None, 'pcol'), may hold values from -0.078125 to 0.078125
- panel: bfloat16 [3, 6, 4, 256, 512], P(None, None, 'prow', 'pcol'), may hold values from -1.1953125 to 1.1953125
- tile_mask: int32 [3, 24], replicated, may hold values 0 or 1
- diag_inverse: float32 [3, 512, 512], P(None, ('prow', 'pcol')), may hold values from -6 to 6
Outputs:
- block_column: bfloat16 [3, 6, 4, 256, 512], P(None, None, 'prow', 'pcol')
- diag_block: float32 [3, 512, 512], P(None, ('prow', 'pcol'))
All inputs are finite; a program needn't handle non-finite values.
Results may differ from a plain program's by a relative error of at most 0.0017.
Values may be sent and summed in bfloat16 or wider, within the bound.
No kernel may reach another device: no remote copies, remote signals or barrier semaphores. Data moves between devices by JAX's collectives and lax.ppermute only.
A program may use at most 128 MiB of HBM per device.

v0:
```python
import jax
import jax.numpy as jnp
from jax import lax
from jax.sharding import PartitionSpec as P


def spread(x, axis, root):
    mine = lax.axis_index(axis) == root
    return lax.psum(jnp.where(mine, x, jnp.zeros_like(x)), axis)


def local_product(anc_block, columns):
    return jnp.einsum("aibj,sbjw->isaw", anc_block, columns, preferred_element_type=jnp.float32)


def outbound(masked, n_row, n_col):
    groups, tile_rows, single, sub_rows, width = masked.shape
    tile_cols = tile_rows * n_row // n_col
    grouped = masked.reshape(groups, tile_cols, n_col // n_row, sub_rows, width)
    return jnp.repeat(grouped, n_row, axis=2)


def body(anc_inverse, panel, tile_mask, diag_inverse):
    n_row = lax.axis_size("prow")
    n_col = lax.axis_size("pcol")
    row_pos = lax.axis_index("prow")
    col_pos = lax.axis_index("pcol")
    sets, tile_rows, single, sub_rows, width = panel.shape
    tiles = tile_mask.shape[1]
    tile_size = anc_inverse.shape[1]
    row_ids = jnp.arange(tile_rows, dtype=jnp.int32) * n_row + row_pos
    hits = (row_ids[:, None] == jnp.arange(tiles, dtype=jnp.int32)[None, :]).astype(jnp.int32)
    row_mask = jnp.sum(tile_mask[:, None, :] * hits[None], axis=2)
    keep = row_mask.astype(jnp.bfloat16)[:, :, None, None, None]
    masked = panel * keep
    outgoing = outbound(masked, n_row, n_col)
    root = col_pos % n_row
    arrived = lax.all_to_all(outgoing, "pcol", split_axis=2, concat_axis=3, tiled=True)
    columns = spread(arrived.reshape(sets, -1, tile_size, width), "prow", root)
    summed = lax.psum_scatter(
        local_product(anc_inverse, columns), "pcol", scatter_dimension=0, tiled=True
    )
    image = -jnp.transpose(summed, (1, 2, 0, 3))[:, :, None] * keep.astype(jnp.float32)
    block_column = image.astype(jnp.bfloat16)
    partial_value = jnp.einsum(
        "saxiw,saxiv->swv", masked, block_column, preferred_element_type=jnp.float32
    )
    mine = lax.psum_scatter(partial_value, ("prow", "pcol"), scatter_dimension=1, tiled=True)
    diag_block = diag_inverse - mine
    return (block_column, diag_block)


def solution(mesh):
    in_specs = (
        P(None, "prow", None, "pcol"),
        P(None, None, "prow", "pcol", None),
        P(),
        P(None, ("prow", "pcol"), None),
    )
    out_specs = (P(None, None, "prow", "pcol", None), P(None, ("prow", "pcol"), None))
    return jax.shard_map(body, mesh=mesh, in_specs=in_specs, out_specs=out_specs, check_vma=False)
```

profile of v0, /device:TPU:0, one launch (start us, length us, event | category | flops | bytes accessed | tf_op | source)
XLA Modules:
  0.0 455.2 jit_solution(3141937686562053441)
XLA Ops:
  7.2 0.1 fusion.6
  7.3 1.0 multiply_reduce_fusion
  8.2 1.2 broadcast_multiply_fusion
  9.4 0.8 copy-done.1
  10.3 1.7 broadcast_in_dim.4
  12.0 6.4 %all-to-all-start = ((bf16[3,3,8,32,512]{4,3,1,0,2:T(8,128)(2,1)}), bf16[3,3,8,32,512]{4,3,1,0,2:T(8,128)(2,1)}, u32[]{:S(2)}, u32[]{:S(2)}) async-start(bf16[3,3,8,32,512]{4,3,1,0,2:T(8,128)(2,1)} %bitcast.27), calls=%async_computation | async-start | bytes 4718592 | tf_op jit(solution)/shard_map/all_to_all | solution.py:38
  18.4 0.0 all-reduce.2.cloned.1.call-start
  18.4 54.7 %all-to-all-done = bf16[3,3,8,32,512]{4,3,1,0,2:T(8,128)(2,1)} async-done(((bf16[3,3,8,32,512]{4,3,1,0,2:T(8,128)(2,1)}), bf16[3,3,8,32,512]{4,3,1,0,2:T(8,128)(2,1)}, u32[]{:S(2)}, u32[]{:S(2)}) %all-to-all-start) | async-done | bytes 2359328 | tf_op jit(solution)/shard_map/all_to_all | solution.py:38
  73.1 3.2 copy_select_fusion
  76.3 4.3 copy.20
  80.6 0.0 all-reduce.2.cloned.1.call-update
  80.6 0.0 reduce-scatter.3.cloned.1.call-start
  80.7 72.9 %all-reduce.2.cloned.1.call-done = bf16[3,3,256,512]{2,3,1,0:T(8,128)(2,1)} async-done(((bf16[3,3,256,512]{2,3,1,0:T(8,128)(2,1)}), bf16[3,3,256,512]{2,3,1,0:T(8,128)(2,1)}) %all-reduce.2.cloned.1.call-update) | async-done | bytes 2359312 | tf_op jit(solution)/shard_map/psum | solution.py:9
  153.6 7.9 %convolution_bitcast_fusion = f32[256,3,6,512]{0,3,2,1:T(8,128)} fusion(bf16[3,3,256,512]{2,3,1,0:T(8,128)(2,1)} %all-reduce.2.cloned.1.call-done, bf16[6,256,3,256]{3,1,2,0:T(8,128)(2,1)S(1)} %copy-done), kind=kOutput, calls=%fused_computation | convolution fusion | flops 3623878656 | bytes 14155776 | tf_op jit(solution)/shard_map/aibj,sbjw->isaw/dot_general | solution.py:13
  161.5 11.9 %copy.21 = f32[256,3,6,512]{3,2,1,0:T(8,128)} copy(f32[256,3,6,512]{0,3,2,1:T(8,128)} %convolution_bitcast_fusion) | data formatting | bytes 18874368 | tf_op jit(solution)/shard_map/aibj,sbjw->isaw/transpose | solution.py:13
  173.4 0.0 reduce-scatter.3.cloned.1.call-update
  173.4 0.0 reduce-scatter.5.cloned.1.call-start
  173.4 129.2 %reduce-scatter.3.cloned.1.call-done = f32[32,3,6,512]{3,2,1,0:T(8,128)} async-done(((f32[256,3,6,512]{3,2,1,0:T(8,128)}), f32[32,3,6,512]{3,2,1,0:T(8,128)}) %reduce-scatter.3.cloned.1.call-update) | async-done | bytes 1179664 | tf_op jit(solution)/shard_map/reduce_scatter | solution.py:40
  302.7 1.8 fusion.5
  304.4 3.4 convolution_bitcast_fusion.1
  307.8 0.0 reduce-scatter.5.cloned.1.call-update
  307.8 1.0 copy.23
  308.8 138.3 %reduce-scatter.5.cloned.1.call-done = f32[3,16,512]{2,1,0:T(8,128)} async-done(((f32[3,512,512]{2,1,0:T(8,128)}), f32[3,16,512]{2,1,0:T(8,128)}) %reduce-scatter.5.cloned.1.call-update) | async-done | bytes 98320 | tf_op jit(solution)/shard_map/reduce_scatter | solution.py:48
  447.1 1.5 sub.3
  (8 shorter events, 0.1 us)
Async XLA Ops:
  7.2 146.4 %copy-start = (bf16[6,256,3,256]{3,1,2,0:T(8,128)(2,1)S(1)}, bf16[6,256,3,256]{3,1,2,0:T(8,128)(2,1)}, u32[]{:S(2)}) copy-start(bf16[6,256,3,256]{3,1,2,0:T(8,128)(2,1)} %param.4) | copy-start | bytes 7077892
  9.4 0.8 copy-start.1
  12.0 61.1 %all-to-all-start = ((bf16[3,3,8,32,512]{4,3,1,0,2:T(8,128)(2,1)}), bf16[3,3,8,32,512]{4,3,1,0,2:T(8,128)(2,1)}, u32[]{:S(2)}, u32[]{:S(2)}) async-start(bf16[3,3,8,32,512]{4,3,1,0,2:T(8,128)(2,1)} %bitcast.27), calls=%async_computation | async-start | bytes 4718592 | tf_op jit(solution)/shard_map/all_to_all | solution.py:38
  18.4 135.2 %all-reduce.2.cloned.1.call-start = ((), (), s32[]{:S(2)}) async-start(), calls=%async_computation.3 | async-start | bytes 4718592 | tf_op jit(solution)/shard_map/psum | solution.py:9
  80.6 222.0 %reduce-scatter.3.cloned.1.call-start = ((), (), s32[]{:S(2)}) async-start(), calls=%async_computation.4 | async-start | bytes 14155776 | tf_op jit(solution)/shard_map/reduce_scatter | solution.py:40
  173.4 273.7 %reduce-scatter.5.cloned.1.call-start = ((), (), s32[]{:S(2)}) async-start(), calls=%async_computation.5 | async-start | bytes 3244032 | tf_op jit(solution)/shard_map/reduce_scatter | solution.py:48
  307.8 139.3 %copy-start.2 = (f32[3,16,512]{2,1,0:T(8,128)S(1)}, f32[3,16,512]{2,1,0:T(8,128)}, u32[]{:S(2)}) copy-start(f32[3,16,512]{2,1,0:T(8,128)} %param.7) | copy-start | bytes 294916
Sparse Core Ops, SparseCore 0:
  80.7 72.7 all-reduce.1
  173.5 129.1 reduce-scatter.2
  308.0 139.0 reduce-scatter.4
where the time goes:
time: 456 us; the launch traced here: 455 us
  waiting for transfers between devices  395 us (87%)
  local copies, waits for them, and re-layouts  19.7 us (4%)
  between operations  13.8 us (3%)
  matrix products  11.3 us (2%)
  other arithmetic  8.76 us (2%)
  starting transfers between devices  6.47 us (1%)
    reduce_scatter x1, waiting for transfers between devices, body(): lax.psum_scatter(partial_value, ('prow', 'pcol'), scatter_dimension=1, ti...  138 us
    reduce_scatter x1, waiting for transfers between devices, body(): lax.psum_scatter(local_product(anc_inverse, columns), 'pcol', scatter_dim...  129 us
    psum x1, waiting for transfers between devices, spread(): return lax.psum(jnp.where(mine, x, jnp.zeros_like(x)), axis)  72.9 us
    all_to_all x1, waiting for transfers between devices, body(): lax.all_to_all(outgoing, 'pcol', split_axis=2, concat_axis=3, tiled=True)  54.7 us
    transpose x1, local copies, waits for them, and re-layouts, local_product(): jnp.einsum('aibj,sbjw->isaw', anc_block, columns, preferred_element_type=...  11.9 us
  transfers between devices with their start and end apart: 4, of which 4 were waited for; matrix products, arithmetic and copies ran while one was open for 0% of the time, Pallas kernels for 0%

commit v1 on v0

v1 whole, which is shorter than its diff:
```python
import jax
import jax.numpy as jnp
from jax import lax
from jax.sharding import PartitionSpec as P

CORES = 2


def line(n_col, senders, step):
    return [
        (z * CORES + c, (z + step) * CORES + c) for z in senders for c in range(CORES)
    ]


def swap(x, n_col):
    return lax.ppermute(x, "pcol", [(q, q ^ 1) for q in range(n_col)])


def gather_rows(x, n_row):
    wide = jnp.broadcast_to(x[None], (n_row,) + x.shape)
    return lax.all_to_all(wide, "prow", 0, 0, tiled=True)


def spread_columns(masked, n_row, n_col):
    sets, tile_rows, sub, width = masked.shape
    tile_cols = tile_rows * n_row // n_col
    n_line = n_col // CORES
    piece = sub // n_row
    x = masked.reshape(sets, tile_rows, n_row, piece, width)
    x = lax.all_to_all(jnp.transpose(x, (2, 0, 1, 3, 4)), "prow", 0, 0, tiled=True)
    x = jnp.transpose(x, (2, 0, 1, 3, 4))
    x = x.reshape(tile_cols, n_line, CORES, sets, piece, CORES, width // CORES)
    x = jnp.transpose(x, (1, 5, 3, 0, 2, 4, 6))
    x = x.reshape((n_col,) + x.shape[2:])
    x = lax.all_to_all(x, "pcol", 0, 0, tiled=True)
    x = gather_rows(x, n_row)
    x = jnp.transpose(x, (2, 3, 4, 1, 0, 5, 6))
    return x.reshape(sets, tile_cols, CORES, n_col * sub, width // CORES)


def reduce_line(partial, place, n_col):
    n_line = n_col // CORES
    shard = lambda k: lax.dynamic_index_in_dim(
        partial, jnp.clip(k, 0, n_line - 1), axis=1, keepdims=False
    )
    up = down = None
    for t in range(1, n_line):
        to_up = shard(place + n_line - t)
        to_down = shard(place - n_line + t)
        if t > 1:
            to_up = to_up + up
            to_down = to_down + down
        up = lax.ppermute(to_up, "pcol", line(n_col, range(t), 1))
        down = lax.ppermute(to_down, "pcol", line(n_col, range(n_line - t, n_line), -1))
    total = shard(place)
    if n_line > 1:
        total = total + up + down
    return total


def reduce_diag(value, n_row, n_col):
    width, half = value.shape
    n_line = n_col // CORES
    x = lax.all_to_all(value.reshape(n_row, width // n_row, half), "prow", 0, 0, tiled=True)
    x = jnp.sum(x, axis=0)
    x = lax.all_to_all(x.reshape(n_col, -1, half), "pcol", 0, 0, tiled=True)
    x = jnp.sum(x.reshape(n_line, CORES, -1, half), axis=0)
    return jnp.transpose(x, (1, 0, 2)).reshape(-1, width)


def body(anc_inverse, panel, tile_mask, diag_inverse):
    n_row = lax.axis_size("prow")
    n_col = lax.axis_size("pcol")
    row_pos = lax.axis_index("prow")
    col_pos = lax.axis_index("pcol")
    place, core = col_pos // CORES, col_pos % CORES
    sets, tile_rows, single, sub, width = panel.shape
    tiles = tile_mask.shape[1]
    n_line = n_col // CORES
    half = width // CORES
    row_ids = jnp.arange(tile_rows, dtype=jnp.int32) * n_row + row_pos
    hits = (row_ids[:, None] == jnp.arange(tiles, dtype=jnp.int32)[None, :]).astype(jnp.int32)
    row_mask = jnp.sum(tile_mask[:, None, :] * hits[None], axis=2)
    keep = row_mask.astype(jnp.bfloat16)[:, :, None, None]
    masked = panel[:, :, 0] * keep
    other_anc = swap(anc_inverse, n_col)
    columns = spread_columns(masked, n_row, n_col)
    other_masked = swap(masked, n_col)
    mine = lax.dynamic_index_in_dim(columns, core, axis=2, keepdims=False)
    others = lax.dynamic_index_in_dim(columns, 1 - core, axis=2, keepdims=False)
    keep32 = keep.astype(jnp.float32)
    blocks, diags = [], []
    for s in range(sets):
        product = jnp.einsum(
            "aibj,bjw->aiw", anc_inverse, mine[s], preferred_element_type=jnp.float32
        ) + jnp.einsum(
            "aibj,bjw->aiw", other_anc, others[s], preferred_element_type=jnp.float32
        )
        partial = product.reshape(tile_rows, n_line, CORES * sub, half)
        total = reduce_line(partial, place, n_col)
        image = (-total * keep32[s]).astype(jnp.bfloat16)
        image = image.reshape(tile_rows, CORES, sub, half)
        stay = lax.dynamic_index_in_dim(image, core, axis=1, keepdims=False)
        leave = lax.dynamic_index_in_dim(image, 1 - core, axis=1, keepdims=False)
        came = swap(leave, n_col)
        low = jnp.where(core == 0, stay, came)
        high = jnp.where(core == 0, came, stay)
        blocks.append(jnp.concatenate([low, high], axis=-1))
        value = jnp.einsum(
            "axw,axv->wv", masked[s], stay, preferred_element_type=jnp.float32
        ) + jnp.einsum(
            "axw,axv->wv", other_masked[s], leave, preferred_element_type=jnp.float32
        )
        diags.append(reduce_diag(value, n_row, n_col))
    block_column = jnp.stack(blocks)[:, :, None]
    diag_block = diag_inverse - jnp.stack(diags)
    return (block_column, diag_block)


def solution(mesh):
    in_specs = (
        P(None, "prow", None, "pcol"),
        P(None, None, "prow", "pcol", None),
        P(),
        P(None, ("prow", "pcol"), None),
    )
    out_specs = (P(None, None, "prow", "pcol", None), P(None, ("prow", "pcol"), None))
    return jax.shard_map(body, mesh=mesh, in_specs=in_specs, out_specs=out_specs, check_vma=False)
```

time: 456 us -> 234 us (0.51)
  waiting for transfers between devices: 395 us -> 92.3 us
  starting transfers between devices: 6.47 us -> 80 us
  blocking collectives: 0 us -> 35.8 us
  local copies, waits for them, and re-layouts: 19.7 us -> 4.9 us
  between operations: 13.8 us -> 1.35 us
    reduce_scatter x2 -> x0, waiting for transfers between devices: 268 us -> none  [the longest x1 138 us: body(): lax.psum_scatter(partial_value, ('prow', 'pcol'), scatter_dimension=1, ti...]
    psum x1 -> x0, waiting for transfers between devices: 72.9 us -> none  [spread(): return lax.psum(jnp.where(mine, x, jnp.zeros_like(x)), axis)]
    ppermute x0 -> x23, starting transfers between devices: none -> 53.2 us  [the longest x9 43.9 us: reduce_line(): up = lax.ppermute(to_up, 'pcol', line(n_col, range(t), 1))]
    all_to_all x0 -> x2, blocking collectives: none -> 35.8 us  [the longest x1 21.4 us: spread_columns(): x = lax.all_to_all(x, 'pcol', 0, 0, tiled=True)]
    ppermute x0 -> x23, waiting for transfers between devices: none -> 33.2 us  [the longest x9 22 us: reduce_line(): up = lax.ppermute(to_up, 'pcol', line(n_col, range(t), 1))]
    all_to_all x1 -> x7, starting transfers between devices: 6.35 us -> 26.9 us  [the longest x3 11.7 us: reduce_diag(): x = lax.all_to_all(x.reshape(n_col, -1, half), 'pcol', 0, 0, tiled=True)]
    transpose x1 -> x6, local copies, waits for them, and re-layouts: 11.9 us -> 2.29 us  [the longest x1 2.1 us: spread_columns(): x = jnp.transpose(x, (2, 3, 4, 1, 0, 5, 6))]
    all_to_all x1 -> x7, waiting for transfers between devices: 54.7 us -> 59.1 us  [the longest x1 27.2 us: gather_rows(): return lax.all_to_all(wide, 'prow', 0, 0, tiled=True)]
  transfers between devices with their start and end apart: 4 -> 30, of which waited for: 4 -> 17; matrix products, arithmetic and copies ran while one was open for 0% -> 7% of each run, Pallas kernels for 0% -> 0%
where the time goes in v1:
time: 234 us; the launch traced here: 233 us
  waiting for transfers between devices  92.3 us (39%)
  starting transfers between devices  80 us (34%)
  blocking collectives  35.8 us (15%)
  matrix products  11.8 us (5%)
  other arithmetic  7.05 us (3%)
  local copies, waits for them, and re-layouts  4.9 us (2%)
    ppermute x9, starting transfers between devices, reduce_line(): up = lax.ppermute(to_up, 'pcol', line(n_col, range(t), 1))  43.9 us
    all_to_all x1, waiting for transfers between devices, gather_rows(): return lax.all_to_all(wide, 'prow', 0, 0, tiled=True)  27.2 us
    ppermute x9, waiting for transfers between devices, reduce_line(): up = lax.ppermute(to_up, 'pcol', line(n_col, range(t), 1))  22 us
    all_to_all x1, blocking collectives, spread_columns(): x = lax.all_to_all(x, 'pcol', 0, 0, tiled=True)  21.4 us
    all_to_all x3, waiting for transfers between devices, reduce_diag(): x = lax.all_to_all(x.reshape(n_col, -1, half), 'pcol', 0, 0, tiled=True)  17.5 us
    all_to_all x3, waiting for transfers between devices, reduce_diag(): lax.all_to_all(value.reshape(n_row, width // n_row, half), 'prow', 0, 0,...  14.4 us
    all_to_all x1, blocking collectives, spread_columns(): lax.all_to_all(jnp.transpose(x, (2, 0, 1, 3, 4)), 'prow', 0, 0, tiled=True)  14.4 us
    all_to_all x3, starting transfers between devices, reduce_diag(): x = lax.all_to_all(x.reshape(n_col, -1, half), 'pcol', 0, 0, tiled=True)  11.7 us
  transfers between devices with their start and end apart: 30, of which 17 were waited for; matrix products, arithmetic and copies ran while one was open for 7% of the time, Pallas kernels for 0%

profile of v1, /device:TPU:0, one launch (start us, length us, event | category | flops | bytes accessed | tf_op | source)
XLA Modules:
  0.0 233.2 jit_solution(3612000978345981846)
XLA Ops:
  2.8 14.4 %all_to_all.45 = bf16[4,3,6,8,512]{4,3,2,1,0:T(8,128)(2,1)S(1)} all-to-all(bf16[4,3,6,8,512]{4,3,2,1,0:T(8,128)(2,1)S(1)} %copy.32), channel_id=1, replica_groups=mesh['prow'=4,'pcol'=8] {'prow'}, dimensions={0} | all-to-all | bytes 1179648 | tf_op jit(solution)/shard_map/all_to_all | solution.py:30
  17.5 21.4 %all_to_all.46 = bf16[8,3,3,2,8,256]{5,4,2,3,1,0:T(8,128)(2,1)S(1)} all-to-all(bf16[8,3,3,2,8,256]{5,4,2,3,1,0:T(8,128)(2,1)S(1)} %bitcast.259), channel_id=1, replica_groups=mesh['prow'=4,'pcol'=8] {'pcol'}, dimensions={0} | all-to-all | bytes 1179648 | tf_op jit(solution)/shard_map/all_to_all | solution.py:35
  40.7 4.6 %all-to-all-start.2 = ((bf16[4,8,3,3,2,8,256]{6,5,1,3,4,2,0:T(8,128)(2,1)}), bf16[4,8,3,3,2,8,256]{6,5,1,3,4,2,0:T(8,128)(2,1)}, u32[]{:S(2)}, u32[]{:S(2)}) async-start(bf16[4,8,3,3,2,8,256]{6,5,1,3,4,2,0:T(8,128)(2,1)} %broadcast_in_dim.4), calls=%async_computation.2 | async-start | bytes 4718592 | tf_op jit(solution)/shard_map/all_to_all | solution.py:21
  46.1 27.2 %all-to-all-done.2 = bf16[4,8,3,3,2,8,256]{6,5,1,3,4,2,0:T(8,128)(2,1)} async-done(((bf16[4,8,3,3,2,8,256]{6,5,1,3,4,2,0:T(8,128)(2,1)}), bf16[4,8,3,3,2,8,256]{6,5,1,3,4,2,0:T(8,128)(2,1)}, u32[]{:S(2)}, u32[]{:S(2)}) %all-to-all-start.2) | async-done | bytes 2359328 | tf_op jit(solution)/shard_map/all_to_all | solution.py:21
  85.9 4.1 %collective-permute-done.15 = f32[6,64,256]{2,1,0:T(8,128)S(1)} collective-permute-done((f32[6,64,256]{2,1,0:T(8,128)S(1)}, f32[6,64,256]{2,1,0:T(8,128)S(1)}, u32[]{:S(2)}, u32[]{:S(2)}) %collective-permute-start.15) | collective-permute-done | bytes 393248 | tf_op jit(solution)/shard_map/ppermute | solution.py:53
  90.0 4.4 %collective-permute-start.8 = (f32[6,64,256]{2,1,0:T(8,128)S(1)}, f32[6,64,256]{2,1,0:T(8,128)S(1)}, u32[]{:S(2)}, u32[]{:S(2)}) collective-permute-start(f32[6,64,256]{2,1,0:T(8,128)S(1)} %get-tuple-element.24), channel_id=1, source_target_pairs={{0,2},{1,3},{8,10},{9,11},{16,18},{17,19},{24,26},{25,27}} | collective-permute-start | bytes 1179656 | tf_op jit(solution)/shard_map/ppermute | solution.py:53
  94.5 4.0 %collective-permute-done.1 = f32[6,64,256]{2,1,0:T(8,128)S(1)} collective-permute-done((f32[6,64,256]{2,1,0:T(8,128)S(1)}, f32[6,64,256]{2,1,0:T(8,128)S(1)}, u32[]{:S(2)}, u32[]{:S(2)}) %collective-permute-start.1) | collective-permute-done | bytes 393248 | tf_op jit(solution)/shard_map/ppermute | solution.py:53
  98.4 4.4 %collective-permute-start.16 = (f32[6,64,256]{2,1,0:T(8,128)S(1)}, f32[6,64,256]{2,1,0:T(8,128)S(1)}, u32[]{:S(2)}, u32[]{:S(2)}) collective-permute-start(f32[6,64,256]{2,1,0:T(8,128)S(1)} %bitcast_add_fusion.5), channel_id=1, source_target_pairs={{0,2},{1,3},{2,4},{3,5},{8,10},{9,11},{10,12},{11,13},{16,18},{17,... | collective-permute-start | bytes 1179656 | tf_op jit(solution)/shard_map/ppermute | solution.py:53
  102.9 4.0 %collective-permute-done.8 = f32[6,64,256]{2,1,0:T(8,128)S(1)} collective-permute-done((f32[6,64,256]{2,1,0:T(8,128)S(1)}, f32[6,64,256]{2,1,0:T(8,128)S(1)}, u32[]{:S(2)}, u32[]{:S(2)}) %collective-permute-start.8) | collective-permute-done | bytes 393248 | tf_op jit(solution)/shard_map/ppermute | solution.py:53
  106.8 4.4 %collective-permute-start.2 = (f32[6,64,256]{2,1,0:T(8,128)S(1)}, f32[6,64,256]{2,1,0:T(8,128)S(1)}, u32[]{:S(2)}, u32[]{:S(2)}) collective-permute-start(f32[6,64,256]{2,1,0:T(8,128)S(1)} %bitcast_add_fusion.15), channel_id=1, source_target_pairs={{0,2},{1,3},{2,4},{3,5},{8,10},{9,11},{10,12},{11,13},{16,18},{17,... | collective-permute-start | bytes 1179656 | tf_op jit(solution)/shard_map/ppermute | solution.py:53
  115.3 4.4 %collective-permute-start.9 = (f32[6,64,256]{2,1,0:T(8,128)S(1)}, f32[6,64,256]{2,1,0:T(8,128)S(1)}, u32[]{:S(2)}, u32[]{:S(2)}) collective-permute-start(f32[6,64,256]{2,1,0:T(8,128)S(1)} %bitcast_add_fusion.10), channel_id=1, source_target_pairs={{0,2},{1,3},{2,4},{3,5},{8,10},{9,11},{10,12},{11,13},{16,18},{17,... | collective-permute-start | bytes 1179656 | tf_op jit(solution)/shard_map/ppermute | solution.py:53
  123.7 4.4 %collective-permute-start.17 = (f32[6,64,256]{2,1,0:T(8,128)S(1)}, f32[6,64,256]{2,1,0:T(8,128)S(1)}, u32[]{:S(2)}, u32[]{:S(2)}) collective-permute-start(f32[6,64,256]{2,1,0:T(8,128)S(1)} %get-tuple-element.26), channel_id=1, source_target_pairs={{0,2},{1,3},{2,4},{3,5},{4,6},{5,7},{8,10},{9,11},{10,12},{11,13},... | collective-permute-start | bytes 1179656 | tf_op jit(solution)/shard_map/ppermute | solution.py:53
  132.1 4.4 %collective-permute-start.3 = (f32[6,64,256]{2,1,0:T(8,128)S(1)}, f32[6,64,256]{2,1,0:T(8,128)S(1)}, u32[]{:S(2)}, u32[]{:S(2)}) collective-permute-start(f32[6,64,256]{2,1,0:T(8,128)S(1)} %get-tuple-element.18), channel_id=1, source_target_pairs={{0,2},{1,3},{2,4},{3,5},{4,6},{5,7},{8,10},{9,11},{10,12},{11,13},... | collective-permute-start | bytes 1179656 | tf_op jit(solution)/shard_map/ppermute | solution.py:53
  140.6 13.9 %collective-permute-start.10 = (f32[6,64,256]{2,1,0:T(8,128)S(1)}, f32[6,64,256]{2,1,0:T(8,128)S(1)}, u32[]{:S(2)}, u32[]{:S(2)}) collective-permute-start(f32[6,64,256]{2,1,0:T(8,128)S(1)} %get-tuple-element.22), channel_id=1, source_target_pairs={{0,2},{1,3},{2,4},{3,5},{4,6},{5,7},{8,10},{9,11},{10,12},{11,13},... | collective-permute-start | bytes 1179656 | tf_op jit(solution)/shard_map/ppermute | solution.py:53
  156.0 5.8 %collective-permute-done.6 = f32[6,64,256]{2,1,0:T(8,128)S(1)} collective-permute-done((f32[6,64,256]{2,1,0:T(8,128)S(1)}, f32[6,64,256]{2,1,0:T(8,128)S(1)}, u32[]{:S(2)}, u32[]{:S(2)}) %collective-permute-start.6) | collective-permute-done | bytes 393248 | tf_op jit(solution)/shard_map/ppermute | solution.py:54
  162.0 4.6 %collective-permute-done.13 = f32[6,64,256]{2,1,0:T(8,128)S(1)} collective-permute-done((f32[6,64,256]{2,1,0:T(8,128)S(1)}, f32[6,64,256]{2,1,0:T(8,128)S(1)}, u32[]{:S(2)}, u32[]{:S(2)}) %collective-permute-start.13) | collective-permute-done | bytes 393248 | tf_op jit(solution)/shard_map/ppermute | solution.py:54
  174.8 4.3 %all-to-all-done.7 = f32[4,128,256]{2,1,0:T(8,128)S(1)} async-done(((f32[4,128,256]{2,1,0:T(8,128)}), f32[4,128,256]{2,1,0:T(8,128)S(1)}, u32[]{:S(2)}, u32[]{:S(2)}) %all-to-all-start.7) | async-done | bytes 524320 | tf_op jit(solution)/shard_map/all_to_all | solution.py:64
  179.2 3.6 %all-to-all-start.5 = ((f32[4,128,256]{2,1,0:T(8,128)}), f32[4,128,256]{2,1,0:T(8,128)S(1)}, u32[]{:S(2)}, u32[]{:S(2)}) async-start(f32[4,128,256]{2,1,0:T(8,128)} %bitcast.92), calls=%async_computation.5 | async-start | bytes 1048576 | tf_op jit(solution)/shard_map/all_to_all | solution.py:64
  185.0 5.6 %all-to-all-done.5 = f32[4,128,256]{2,1,0:T(8,128)S(1)} async-done(((f32[4,128,256]{2,1,0:T(8,128)}), f32[4,128,256]{2,1,0:T(8,128)S(1)}, u32[]{:S(2)}, u32[]{:S(2)}) %all-to-all-start.5) | async-done | bytes 524320 | tf_op jit(solution)/shard_map/all_to_all | solution.py:64
  196.2 4.5 %all-to-all-done.3 = f32[4,128,256]{2,1,0:T(8,128)S(1)} async-done(((f32[4,128,256]{2,1,0:T(8,128)}), f32[4,128,256]{2,1,0:T(8,128)S(1)}, u32[]{:S(2)}, u32[]{:S(2)}) %all-to-all-start.3) | async-done | bytes 524320 | tf_op jit(solution)/shard_map/all_to_all | solution.py:64
  200.6 5.0 %all-to-all-start.8 = ((f32[8,16,256]{2,1,0:T(8,128)}), f32[8,16,256]{2,1,0:T(8,128)S(1)}, u32[]{:S(2)}, u32[]{:S(2)}) async-start(f32[8,16,256]{2,1,0:T(8,128)} %bitcast.101), calls=%async_computation.8 | async-start | bytes 262144 | tf_op jit(solution)/shard_map/all_to_all | solution.py:66
  206.4 6.0 %all-to-all-done.8 = f32[8,16,256]{2,1,0:T(8,128)S(1)} async-done(((f32[8,16,256]{2,1,0:T(8,128)}), f32[8,16,256]{2,1,0:T(8,128)S(1)}, u32[]{:S(2)}, u32[]{:S(2)}) %all-to-all-start.8) | async-done | bytes 131104 | tf_op jit(solution)/shard_map/all_to_all | solution.py:66
  216.5 6.0 %all-to-all-done.6 = f32[8,16,256]{2,1,0:T(8,128)S(1)} async-done(((f32[8,16,256]{2,1,0:T(8,128)}), f32[8,16,256]{2,1,0:T(8,128)S(1)}, u32[]{:S(2)}, u32[]{:S(2)}) %all-to-all-start.6) | async-done | bytes 131104 | tf_op jit(solution)/shard_map/all_to_all | solution.py:66
  226.9 5.6 %all-to-all-done.4 = f32[8,16,256]{2,1,0:T(8,128)S(1)} async-done(((f32[8,16,256]{2,1,0:T(8,128)}), f32[8,16,256]{2,1,0:T(8,128)S(1)}, u32[]{:S(2)}, u32[]{:S(2)}) %all-to-all-start.4) | async-done | bytes 131104 | tf_op jit(solution)/shard_map/all_to_all | solution.py:66
  (111 shorter events, 61.1 us)
Async XLA Ops:
  40.7 32.6 %all-to-all-start.2 = ((bf16[4,8,3,3,2,8,256]{6,5,1,3,4,2,0:T(8,128)(2,1)}), bf16[4,8,3,3,2,8,256]{6,5,1,3,4,2,0:T(8,128)(2,1)}, u32[]{:S(2)}, u32[]{:S(2)}) async-start(bf16[4,8,3,3,2,8,256]{6,5,1,3,4,2,0:T(8,128)(2,1)} %broadcast_in_dim.4), calls=%async_computation.2 | async-start | bytes 4718592 | tf_op jit(solution)/shard_map/all_to_all | solution.py:21
  45.3 32.0 %collective-permute-start = (bf16[6,256,3,256]{3,1,2,0:T(8,128)(2,1)}, bf16[6,256,3,256]{3,1,2,0:T(8,128)(2,1)S(1)}, u32[]{:S(2)}, u32[]{:S(2)}) collective-permute-start(bf16[6,256,3,256]{3,1,2,0:T(8,128)(2,1)} %param.4), channel_id=1, source_target_pairs={{0,1},{1,0},{2,3},{3,2},{4,5},{5,4},{6,7},{7,6},{8,9},{9,8},{10,11... | collective-permute-start | bytes 7077896 | tf_op jit(solution)/shard_map/ppermute | solution.py:16
  45.5 121.5 %collective-permute-start.22 = (bf16[3,6,32,512]{3,2,1,0:T(8,128)(2,1)S(1)}, bf16[3,6,32,512]{3,2,1,0:T(8,128)(2,1)}, u32[]{:S(2)}, u32[]{:S(2)}) collective-permute-start(bf16[3,6,32,512]{3,2,1,0:T(8,128)(2,1)S(1)} %bitcast_multiply_fusion), channel_id=1, source_target_pairs={{0,1},{1,0},{2,3},{3,2},{4,5},{5,4},{6,7},{7,6},{8,9},{9,8},{10,11... | collective-permute-start | bytes 1769480 | tf_op jit(solution)/shard_map/ppermute | solution.py:16
  78.2 11.7 %collective-permute-start.15 = (f32[6,64,256]{2,1,0:T(8,128)S(1)}, f32[6,64,256]{2,1,0:T(8,128)S(1)}, u32[]{:S(2)}, u32[]{:S(2)}) collective-permute-start(f32[6,64,256]{2,1,0:T(8,128)S(1)} %get-tuple-element.28), channel_id=1, source_target_pairs={{0,2},{1,3},{8,10},{9,11},{16,18},{17,19},{24,26},{25,27}} | collective-permute-start | bytes 1179656 | tf_op jit(solution)/shard_map/ppermute | solution.py:53
  80.5 30.8 %collective-permute-start.18 = (f32[6,64,256]{2,1,0:T(8,128)S(1)}, f32[6,64,256]{2,1,0:T(8,128)S(1)}, u32[]{:S(2)}, u32[]{:S(2)}) collective-permute-start(f32[6,64,256]{2,1,0:T(8,128)S(1)} %get-tuple-element.29), channel_id=1, source_target_pairs={{6,4},{7,5},{14,12},{15,13},{22,20},{23,21},{30,28},{31,29}} | collective-permute-start | bytes 1179656 | tf_op jit(solution)/shard_map/ppermute | solution.py:54
  82.2 16.2 %collective-permute-start.1 = (f32[6,64,256]{2,1,0:T(8,128)S(1)}, f32[6,64,256]{2,1,0:T(8,128)S(1)}, u32[]{:S(2)}, u32[]{:S(2)}) collective-permute-start(f32[6,64,256]{2,1,0:T(8,128)S(1)} %get-tuple-element.20), channel_id=1, source_target_pairs={{0,2},{1,3},{8,10},{9,11},{16,18},{17,19},{24,26},{25,27}} | collective-permute-start | bytes 1179656 | tf_op jit(solution)/shard_map/ppermute | solution.py:53
  83.5 36.3 %collective-permute-start.4 = (f32[6,64,256]{2,1,0:T(8,128)S(1)}, f32[6,64,256]{2,1,0:T(8,128)S(1)}, u32[]{:S(2)}, u32[]{:S(2)}) collective-permute-start(f32[6,64,256]{2,1,0:T(8,128)S(1)} %get-tuple-element.21), channel_id=1, source_target_pairs={{6,4},{7,5},{14,12},{15,13},{22,20},{23,21},{30,28},{31,29}} | collective-permute-start | bytes 1179656 | tf_op jit(solution)/shard_map/ppermute | solution.py:54
  90.0 16.9 %collective-permute-start.8 = (f32[6,64,256]{2,1,0:T(8,128)S(1)}, f32[6,64,256]{2,1,0:T(8,128)S(1)}, u32[]{:S(2)}, u32[]{:S(2)}) collective-permute-start(f32[6,64,256]{2,1,0:T(8,128)S(1)} %get-tuple-element.24), channel_id=1, source_target_pairs={{0,2},{1,3},{8,10},{9,11},{16,18},{17,19},{24,26},{25,27}} | collective-permute-start | bytes 1179656 | tf_op jit(solution)/shard_map/ppermute | solution.py:53
  98.4 16.9 %collective-permute-start.16 = (f32[6,64,256]{2,1,0:T(8,128)S(1)}, f32[6,64,256]{2,1,0:T(8,128)S(1)}, u32[]{:S(2)}, u32[]{:S(2)}) collective-permute-start(f32[6,64,256]{2,1,0:T(8,128)S(1)} %bitcast_add_fusion.5), channel_id=1, source_target_pairs={{0,2},{1,3},{2,4},{3,5},{8,10},{9,11},{10,12},{11,13},{16,18},{17,... | collective-permute-start | bytes 1179656 | tf_op jit(solution)/shard_map/ppermute | solution.py:53
  106.8 16.9 %collective-permute-start.2 = (f32[6,64,256]{2,1,0:T(8,128)S(1)}, f32[6,64,256]{2,1,0:T(8,128)S(1)}, u32[]{:S(2)}, u32[]{:S(2)}) collective-permute-start(f32[6,64,256]{2,1,0:T(8,128)S(1)} %bitcast_add_fusion.15), channel_id=1, source_target_pairs={{0,2},{1,3},{2,4},{3,5},{8,10},{9,11},{10,12},{11,13},{16,18},{17,... | collective-permute-start | bytes 1179656 | tf_op jit(solution)/shard_map/ppermute | solution.py:53
  111.3 16.9 %collective-permute-start.11 = (f32[6,64,256]{2,1,0:T(8,128)S(1)}, f32[6,64,256]{2,1,0:T(8,128)S(1)}, u32[]{:S(2)}, u32[]{:S(2)}) collective-permute-start(f32[6,64,256]{2,1,0:T(8,128)S(1)} %get-tuple-element.25), channel_id=1, source_target_pairs={{6,4},{7,5},{14,12},{15,13},{22,20},{23,21},{30,28},{31,29}} | collective-permute-start | bytes 1179656 | tf_op jit(solution)/shard_map/ppermute | solution.py:54
  115.3 16.9 %collective-permute-start.9 = (f32[6,64,256]{2,1,0:T(8,128)S(1)}, f32[6,64,256]{2,1,0:T(8,128)S(1)}, u32[]{:S(2)}, u32[]{:S(2)}) collective-permute-start(f32[6,64,256]{2,1,0:T(8,128)S(1)} %bitcast_add_fusion.10), channel_id=1, source_target_pairs={{0,2},{1,3},{2,4},{3,5},{8,10},{9,11},{10,12},{11,13},{16,18},{17,... | collective-permute-start | bytes 1179656 | tf_op jit(solution)/shard_map/ppermute | solution.py:53
  119.8 16.9 %collective-permute-start.19 = (f32[6,64,256]{2,1,0:T(8,128)S(1)}, f32[6,64,256]{2,1,0:T(8,128)S(1)}, u32[]{:S(2)}, u32[]{:S(2)}) collective-permute-start(f32[6,64,256]{2,1,0:T(8,128)S(1)} %get-tuple-element.27), channel_id=1, source_target_pairs={{4,2},{5,3},{6,4},{7,5},{12,10},{13,11},{14,12},{15,13},{20,18},{2... | collective-permute-start | bytes 1179656 | tf_op jit(solution)/shard_map/ppermute | solution.py:54
  123.7 16.9 %collective-permute-start.17 = (f32[6,64,256]{2,1,0:T(8,128)S(1)}, f32[6,64,256]{2,1,0:T(8,128)S(1)}, u32[]{:S(2)}, u32[]{:S(2)}) collective-permute-start(f32[6,64,256]{2,1,0:T(8,128)S(1)} %get-tuple-element.26), channel_id=1, source_target_pairs={{0,2},{1,3},{2,4},{3,5},{4,6},{5,7},{8,10},{9,11},{10,12},{11,13},... | collective-permute-start | bytes 1179656 | tf_op jit(solution)/shard_map/ppermute | solution.py:53
  132.1 23.9 %collective-permute-start.3 = (f32[6,64,256]{2,1,0:T(8,128)S(1)}, f32[6,64,256]{2,1,0:T(8,128)S(1)}, u32[]{:S(2)}, u32[]{:S(2)}) collective-permute-start(f32[6,64,256]{2,1,0:T(8,128)S(1)} %get-tuple-element.18), channel_id=1, source_target_pairs={{0,2},{1,3},{2,4},{3,5},{4,6},{5,7},{8,10},{9,11},{10,12},{11,13},... | collective-permute-start | bytes 1179656 | tf_op jit(solution)/shard_map/ppermute | solution.py:53
  137.4 17.0 %collective-permute-start.20 = (f32[6,64,256]{2,1,0:T(8,128)S(1)}, f32[6,64,256]{2,1,0:T(8,128)S(1)}, u32[]{:S(2)}, u32[]{:S(2)}) collective-permute-start(f32[6,64,256]{2,1,0:T(8,128)S(1)} %bitcast_add_fusion.4), channel_id=1, source_target_pairs={{2,0},{3,1},{4,2},{5,3},{6,4},{7,5},{10,8},{11,9},{12,10},{13,11},... | collective-permute-start | bytes 1179656 | tf_op jit(solution)/shard_map/ppermute | solution.py:54
  138.8 23.0 %collective-permute-start.6 = (f32[6,64,256]{2,1,0:T(8,128)S(1)}, f32[6,64,256]{2,1,0:T(8,128)S(1)}, u32[]{:S(2)}, u32[]{:S(2)}) collective-permute-start(f32[6,64,256]{2,1,0:T(8,128)S(1)} %bitcast_add_fusion.14), channel_id=1, source_target_pairs={{2,0},{3,1},{4,2},{5,3},{6,4},{7,5},{10,8},{11,9},{12,10},{13,11},... | collective-permute-start | bytes 1179656 | tf_op jit(solution)/shard_map/ppermute | solution.py:54
  140.6 21.4 %collective-permute-start.10 = (f32[6,64,256]{2,1,0:T(8,128)S(1)}, f32[6,64,256]{2,1,0:T(8,128)S(1)}, u32[]{:S(2)}, u32[]{:S(2)}) collective-permute-start(f32[6,64,256]{2,1,0:T(8,128)S(1)} %get-tuple-element.22), channel_id=1, source_target_pairs={{0,2},{1,3},{2,4},{3,5},{4,6},{5,7},{8,10},{9,11},{10,12},{11,13},... | collective-permute-start | bytes 1179656 | tf_op jit(solution)/shard_map/ppermute | solution.py:53
  154.5 12.1 %collective-permute-start.13 = (f32[6,64,256]{2,1,0:T(8,128)S(1)}, f32[6,64,256]{2,1,0:T(8,128)S(1)}, u32[]{:S(2)}, u32[]{:S(2)}) collective-permute-start(f32[6,64,256]{2,1,0:T(8,128)S(1)} %bitcast_add_fusion.9), channel_id=1, source_target_pairs={{2,0},{3,1},{4,2},{5,3},{6,4},{7,5},{10,8},{11,9},{12,10},{13,11},... | collective-permute-start | bytes 1179656 | tf_op jit(solution)/shard_map/ppermute | solution.py:54
  169.1 10.1 %all-to-all-start.7 = ((f32[4,128,256]{2,1,0:T(8,128)}), f32[4,128,256]{2,1,0:T(8,128)S(1)}, u32[]{:S(2)}, u32[]{:S(2)}) async-start(f32[4,128,256]{2,1,0:T(8,128)} %bitcast.100), calls=%async_computation.7 | async-start | bytes 1048576 | tf_op jit(solution)/shard_map/all_to_all | solution.py:64
  179.2 11.5 %all-to-all-start.5 = ((f32[4,128,256]{2,1,0:T(8,128)}), f32[4,128,256]{2,1,0:T(8,128)S(1)}, u32[]{:S(2)}, u32[]{:S(2)}) async-start(f32[4,128,256]{2,1,0:T(8,128)} %bitcast.92), calls=%async_computation.5 | async-start | bytes 1048576 | tf_op jit(solution)/shard_map/all_to_all | solution.py:64
  194.2 21.5 %collective-permute-start.21 = (bf16[6,32,256]{2,1,0:T(8,128)(2,1)S(1)}, bf16[6,32,256]{2,1,0:T(8,128)(2,1)S(1)}, u32[]{:S(2)}, u32[]{:S(2)}) collective-permute-start(bf16[6,32,256]{2,1,0:T(8,128)(2,1)S(1)} %copy-done.3), channel_id=1, source_target_pairs={{0,1},{1,0},{2,3},{3,2},{4,5},{5,4},{6,7},{7,6},{8,9},{9,8},{10,11... | collective-permute-start | bytes 294920 | tf_op jit(solution)/shard_map/ppermute | solution.py:16
  194.7 10.9 %collective-permute-start.14 = (bf16[6,32,256]{2,1,0:T(8,128)(2,1)S(1)}, bf16[6,32,256]{2,1,0:T(8,128)(2,1)S(1)}, u32[]{:S(2)}, u32[]{:S(2)}) collective-permute-start(bf16[6,32,256]{2,1,0:T(8,128)(2,1)S(1)} %dynamic-slice_bitcast_fusion.19), channel_id=1, source_target_pairs={{0,1},{1,0},{2,3},{3,2},{4,5},{5,4},{6,7},{7,6},{8,9},{9,8},{10,11... | collective-permute-start | bytes 294920 | tf_op jit(solution)/shard_map/ppermute | solution.py:16
  200.6 11.7 %all-to-all-start.8 = ((f32[8,16,256]{2,1,0:T(8,128)}), f32[8,16,256]{2,1,0:T(8,128)S(1)}, u32[]{:S(2)}, u32[]{:S(2)}) async-start(f32[8,16,256]{2,1,0:T(8,128)} %bitcast.101), calls=%async_computation.8 | async-start | bytes 262144 | tf_op jit(solution)/shard_map/all_to_all | solution.py:66
  (11 other events, 105.0 us)

commit v2 on v0

v2 whole, which is shorter than its diff:
```python
import functools

import jax
import jax.numpy as jnp
from jax import lax
from jax.experimental import pallas as pl
from jax.experimental.pallas import tpu as pltpu
from jax.sharding import PartitionSpec as P


CORES = 2
CHUNKS = 3


def by_col(x, n_col, k):
    return lax.ppermute(x, "pcol", [(q, q ^ k) for q in range(n_col)])


def by_row(x, n_row, k):
    return lax.ppermute(x, "prow", [(p, p ^ k) for p in range(n_row)])


def pick(x, index, axis):
    return lax.dynamic_index_in_dim(x, index, axis=axis, keepdims=False)


def product_kernel(counts, groups, pos, *refs):
    n_row = len(counts)
    refs, rest = refs[: sum(counts)], refs[sum(counts) :]
    blocks = []
    for count in counts:
        blocks.append(refs[:count])
        refs = refs[count:]
    pieces, outs, held = rest[:n_row], rest[n_row : n_row + groups], rest[n_row + groups]
    place, group, turn = pos[0], pos[1], pos[2]
    n_line, tile_cols, rows, _ = pieces[0].shape
    tile = n_line * rows
    for k in range(n_row):
        for j in range(n_line):
            start = pl.multiple_of((place ^ j) * rows, rows)
            for b in range(tile_cols):
                part = (k ^ turn) * tile_cols + b
                held[pl.ds(pl.multiple_of(part * tile, tile) + start, rows), :] = pieces[k][j, b]

    def left(block, b, r):
        parts = [x[:, b, group ^ r].reshape(x.shape[0] * rows, tile) for x in block]
        return parts[0] if len(parts) == 1 else jnp.concatenate(parts, axis=0)

    for r in reversed(range(groups)):
        wide = jnp.concatenate(
            [left(block, b, r) for block in blocks for b in range(tile_cols)], axis=1
        )
        outs[r][...] = jnp.dot(wide, held[...], preferred_element_type=jnp.float32)


def product(pos, blocks, pieces):
    n_row = len(blocks)
    _, tile_cols, groups, rows, tile = blocks[0][0].shape
    half = pieces[0].shape[-1]
    height = sum(x.shape[0] for x in blocks[0]) * rows
    depth = n_row * tile_cols * tile
    flat = [x for block in blocks for x in block]
    vmem = pl.BlockSpec(memory_space=pltpu.VMEM)
    return pl.pallas_call(
        functools.partial(product_kernel, tuple(len(block) for block in blocks), groups),
        out_shape=[jax.ShapeDtypeStruct((height, half), jnp.float32)] * groups,
        in_specs=[pl.BlockSpec(memory_space=pltpu.SMEM)] + [vmem] * (len(flat) + n_row),
        out_specs=[vmem] * groups,
        scratch_shapes=[pltpu.VMEM((depth, half), jnp.bfloat16)],
        cost_estimate=pl.CostEstimate(
            flops=2 * groups * height * depth * half,
            bytes_accessed=2 * depth * (groups * height + half) + 4 * groups * height * half,
            transcendentals=0,
        ),
    )(pos, *flat, *pieces)


def share_panel(x, group, groups, members, n_col):
    got = [pick(x, group, 1)]
    for k in range(1, groups):
        got.append(by_col(pick(x, group ^ k, 1), n_col, k * members * CORES))
    got = jnp.stack(got)
    all_got = [got] + [by_col(got, n_col, m * CORES) for m in range(1, members)]
    return jnp.stack(all_got, axis=1).reshape((-1,) + got.shape[1:])


def reduce_groups(parts, groups, members, n_col):
    k = 1
    while k < groups:
        parts = [
            parts[r] + by_col(parts[r + 1], n_col, k * members * CORES)
            for r in range(0, len(parts), 2)
        ]
        k *= 2
    return parts[0]


def reduce_diag(value, n_row, n_col):
    width, half = value.shape
    n_line = n_col // CORES
    x = lax.all_to_all(value.reshape(n_row, width // n_row, half), "prow", 0, 0, tiled=True)
    x = jnp.sum(x, axis=0)
    x = lax.all_to_all(x.reshape(n_col, -1, half), "pcol", 0, 0, tiled=True)
    x = jnp.sum(x.reshape(n_line, CORES, -1, half), axis=0)
    return jnp.transpose(x, (1, 0, 2)).reshape(-1, width)


def step(anc_inverse, panel, tile_mask, diag_inverse):
    n_row = lax.axis_size("prow")
    n_col = lax.axis_size("pcol")
    row_pos = lax.axis_index("prow")
    col_pos = lax.axis_index("pcol")
    place, core = col_pos // CORES, col_pos % CORES
    sets, tile_rows, _, sub, width = panel.shape
    tiles = tile_mask.shape[1]
    n_line = n_col // CORES
    members = n_row // CORES
    groups = n_line // members
    group, within = place // members, place % members
    half = width // CORES
    row_ids = jnp.arange(tile_rows, dtype=jnp.int32) * n_row + row_pos
    hits = (row_ids[:, None] == jnp.arange(tiles, dtype=jnp.int32)[None, :]).astype(jnp.int32)
    row_mask = jnp.sum(tile_mask[:, None, :] * hits[None], axis=2)
    keep = row_mask.astype(jnp.bfloat16)[:, :, None, None]
    keep32 = keep.astype(jnp.float32)
    masked = panel[:, :, 0] * keep
    tile_cols = tile_rows // groups
    anc = jnp.transpose(anc_inverse, (0, 2, 1, 3))
    anc = anc.reshape(tile_rows, tile_cols, groups, members, CORES * sub, -1)
    count = CHUNKS if tile_rows % CHUNKS == 0 else 1
    own = [pick(anc, within, 3)]
    blocks = [own, [by_col(own[0], n_col, 1)]]
    for m in range(1, members):
        there, across = [], []
        for x in jnp.split(pick(anc, within ^ m, 3), count):
            there.append(by_col(x, n_col, m * CORES))
            across.append(by_col(there[-1], n_col, 1))
        blocks += [there, across]
    other = by_col(masked, n_col, 1)
    both = jnp.concatenate(
        [jnp.where(core == 0, masked, other), jnp.where(core == 0, other, masked)], axis=2
    )
    narrow = lax.dynamic_slice_in_dim(both, core * half, half, axis=3)
    narrow = narrow.reshape(sets, tile_cols, groups, CORES * sub, half)
    pos = jnp.stack([place, group, row_pos ^ (col_pos % n_row)]).astype(jnp.int32)
    outs, diags = [], []
    for s in range(sets):
        piece = share_panel(narrow[s], group, groups, members, n_col)
        pieces = [piece] + [by_row(piece, n_row, k) for k in range(1, n_row)]
        parts = product(pos, blocks, pieces)
        total = reduce_groups(parts, groups, members, n_col)
        total = total.reshape(tile_rows, CORES, sub, half)
        image = (-total * keep32[s, :, None]).astype(jnp.bfloat16)
        stay, leave = pick(image, core, 1), pick(image, 1 - core, 1)
        came = by_col(leave, n_col, 1)
        outs.append(
            jnp.concatenate(
                [jnp.where(core == 0, stay, came), jnp.where(core == 0, came, stay)], axis=-1
            )
        )
        value = jnp.einsum(
            "axw,axv->wv", both[s], image.reshape(tile_rows, -1, half),
            preferred_element_type=jnp.float32,
        )
        diags.append(reduce_diag(value, n_row, n_col))
    block_column = jnp.stack(outs)[:, :, None]
    diag_block = diag_inverse - jnp.stack(diags)
    return (block_column, diag_block)


def solution(mesh):
    in_specs = (
        P(None, "prow", None, "pcol"),
        P(None, None, "prow", "pcol", None),
        P(),
        P(None, ("prow", "pcol"), None),
    )
    out_specs = (P(None, None, "prow", "pcol", None), P(None, ("prow", "pcol"), None))
    return jax.shard_map(step, mesh=mesh, in_specs=in_specs, out_specs=out_specs, check_vma=False)
```

time: 456 us -> 196 us (0.43)
  waiting for transfers between devices: 395 us -> 94.4 us
  starting transfers between devices: 6.47 us -> 57.6 us
  Pallas kernels: 0 us -> 15.5 us
  local copies, waits for them, and re-layouts: 19.7 us -> 6.1 us
  between operations: 13.8 us -> 1.08 us
  other arithmetic: 8.76 us -> 17 us
  matrix products: 11.3 us -> 3.42 us
    reduce_scatter x2 -> x0, waiting for transfers between devices: 268 us -> none  [the longest x1 138 us: body(): lax.psum_scatter(partial_value, ('prow', 'pcol'), scatter_dimension=1, ti...]
    psum x1 -> x0, waiting for transfers between devices: 72.9 us -> none  [spread(): return lax.psum(jnp.where(mine, x, jnp.zeros_like(x)), axis)]
    ppermute x0 -> x29, waiting for transfers between devices: none -> 64.8 us  [the longest x20 44 us: by_col(): return lax.ppermute(x, 'pcol', [(q, q ^ k) for q in range(n_col)])]
    ppermute x0 -> x29, starting transfers between devices: none -> 36.3 us  [the longest x20 22.1 us: by_col(): return lax.ppermute(x, 'pcol', [(q, q ^ k) for q in range(n_col)])]
    all_to_all x1 -> x6, waiting for transfers between devices: 54.7 us -> 29.6 us  [the longest x3 16.6 us: reduce_diag(): x = lax.all_to_all(x.reshape(n_col, -1, half), 'pcol', 0, 0, tiled=True)]
    pallas_call x0 -> x3, Pallas kernels: none -> 15.5 us  [product(): pl.pallas_call(functools.partial(product_kernel, tuple((len(block) for bl...]
    all_to_all x1 -> x6, starting transfers between devices: 6.35 us -> 21.3 us  [the longest x3 10.7 us: reduce_diag(): x = lax.all_to_all(x.reshape(n_col, -1, half), 'pcol', 0, 0, tiled=True)]
    transpose x1 -> x3, local copies, waits for them, and re-layouts: 11.9 us -> 0.08 us  [reduce_diag(): return jnp.transpose(x, (1, 0, 2)).reshape(-1, width)]
  transfers between devices with their start and end apart: 4 -> 35, of which waited for: 4 -> 18; matrix products, arithmetic and copies ran while one was open for 0% -> 11% of each run, Pallas kernels for 0% -> 8%
where the time goes in v2:
time: 196 us; the launch traced here: 195 us
  waiting for transfers between devices  94.4 us (48%)
  starting transfers between devices  57.6 us (29%)
  other arithmetic  17 us (9%)
  Pallas kernels  15.5 us (8%)
  local copies, waits for them, and re-layouts  6.1 us (3%)
  matrix products  3.42 us (2%)
    ppermute x20, waiting for transfers between devices, by_col(): return lax.ppermute(x, 'pcol', [(q, q ^ k) for q in range(n_col)])  44 us
    ppermute x20, starting transfers between devices, by_col(): return lax.ppermute(x, 'pcol', [(q, q ^ k) for q in range(n_col)])  22.1 us
    ppermute x9, waiting for transfers between devices, by_row(): return lax.ppermute(x, 'prow', [(p, p ^ k) for p in range(n_row)])  20.8 us
    all_to_all x3, waiting for transfers between devices, reduce_diag(): x = lax.all_to_all(x.reshape(n_col, -1, half), 'pcol', 0, 0, tiled=True)  16.6 us
    pallas_call x3, Pallas kernels, product(): pl.pallas_call(functools.partial(product_kernel, tuple((len(block) for bl...  15.5 us
    ppermute x9, starting transfers between devices, by_row(): return lax.ppermute(x, 'prow', [(p, p ^ k) for p in range(n_row)])  14.2 us
    all_to_all x3, waiting for transfers between devices, reduce_diag(): lax.all_to_all(value.reshape(n_row, width // n_row, half), 'prow', 0, 0,...  12.9 us
    all_to_all x3, starting transfers between devices, reduce_diag(): x = lax.all_to_all(x.reshape(n_col, -1, half), 'pcol', 0, 0, tiled=True)  10.7 us
  transfers between devices with their start and end apart: 35, of which 18 were waited for; matrix products, arithmetic and copies ran while one was open for 11% of the time, Pallas kernels for 8%

profile of v2, /device:TPU:0, one launch (start us, length us, event | category | flops | bytes accessed | tf_op | source)
XLA Modules:
  0.0 195.0 jit_solution(373224427451987537)
XLA Ops:
  11.5 7.8 %collective-permute-done.1.refs_2_ = bf16[2,3,2,64,256]{4,3,2,1,0:T(8,128)(2,1)} collective-permute-done((bf16[2,3,2,64,256]{4,3,2,1,0:T(8,128)(2,1)}, bf16[2,3,2,64,256]{4,3,2,1,0:T(8,128)(2,1)}, u32[]{:S(2)}, u32[]{:S(2)}) %collective-permute-start.1) | collective-permute-done | bytes 393248 | tf_op jit(solution)/shard_map/ppermute | solution.py:16
  24.0 5.9 %collective-permute-done.2.refs_3_ = bf16[2,3,2,64,256]{4,3,2,1,0:T(8,128)(2,1)} collective-permute-done((bf16[2,3,2,64,256]{4,3,2,1,0:T(8,128)(2,1)}, bf16[2,3,2,64,256]{4,3,2,1,0:T(8,128)(2,1)}, u32[]{:S(2)}, u32[]{:S(2)}) %collective-permute-start.2) | collective-permute-done | bytes 393248 | tf_op jit(solution)/shard_map/ppermute | solution.py:16
  32.0 8.2 %collective-permute-done.3.refs_4_ = bf16[2,3,2,64,256]{4,3,2,1,0:T(8,128)(2,1)} collective-permute-done((bf16[2,3,2,64,256]{4,3,2,1,0:T(8,128)(2,1)}, bf16[2,3,2,64,256]{4,3,2,1,0:T(8,128)(2,1)}, u32[]{:S(2)}, u32[]{:S(2)}) %collective-permute-start.3) | collective-permute-done | bytes 393248 | tf_op jit(solution)/shard_map/ppermute | solution.py:16
  42.8 5.7 %collective-permute-done.22 = bf16[3,64,256]{2,1,0:T(8,128)(2,1)S(1)} collective-permute-done((bf16[3,64,256]{2,1,0:T(8,128)(2,1)S(1)}, bf16[3,64,256]{2,1,0:T(8,128)(2,1)S(1)}, u32[]{:S(2)}, u32[]{:S(2)}) %collective-permute-start.22) | collective-permute-done | bytes 98336 | tf_op jit(solution)/shard_map/ppermute | solution.py:16
  51.4 4.7 %collective-permute-done.16 = bf16[2,3,64,256]{3,2,1,0:T(8,128)(2,1)S(1)} collective-permute-done((bf16[2,3,64,256]{3,2,1,0:T(8,128)(2,1)S(1)}, bf16[2,3,64,256]{3,2,1,0:T(8,128)(2,1)S(1)}, u32[]{:S(2)}, u32[]{:S(2)}) %collective-permute-start.16) | collective-permute-done | bytes 196640 | tf_op jit(solution)/shard_map/ppermute | solution.py:16
  72.0 7.0 %collective-permute-done.18.refs_10_ = bf16[4,3,64,256]{3,2,1,0:T(8,128)(2,1)} collective-permute-done((bf16[4,3,64,256]{3,2,1,0:T(8,128)(2,1)}, bf16[4,3,64,256]{3,2,1,0:T(8,128)(2,1)}, u32[]{:S(2)}, u32[]{:S(2)}) %collective-permute-start.18) | collective-permute-done | bytes 393248 | tf_op jit(solution)/shard_map/ppermute | solution.py:20
  81.0 5.1 %shard_map.60 = (f32[384,256]{1,0:T(8,128)}, f32[384,256]{1,0:T(8,128)}) custom-call(s32[3]{0:T(128)} %pad_add_fusion.pos, bf16[6,3,2,64,256]{4,3,2,1,0:T(8,128)(2,1)} %copy-done, bf16[6,3,2,64,256]{4,3,2,1,0:T(8,128)(2,1)} %copy-done.1, bf16[2,3,2,64,256]{4,3,2,1,0:T(8,128)(2,1)} %collective-permute-done.1.refs_2_, ...), custom_call_target="tpu_custom_call" | custom-call | flops 1207959552 | bytes 7077888 | tf_op jit(solution)/shard_map/pallas_call | solution.py:64
  88.9 6.9 %collective-permute-done.11.refs_10_ = bf16[4,3,64,256]{3,2,1,0:T(8,128)(2,1)S(1)} collective-permute-done((bf16[4,3,64,256]{3,2,1,0:T(8,128)(2,1)}, bf16[4,3,64,256]{3,2,1,0:T(8,128)(2,1)S(1)}, u32[]{:S(2)}, u32[]{:S(2)}) %collective-permute-start.11) | collective-permute-done | bytes 393248 | tf_op jit(solution)/shard_map/ppermute | solution.py:20
  99.6 5.2 %shard_map.59 = (f32[384,256]{1,0:T(8,128)}, f32[384,256]{1,0:T(8,128)}) custom-call(s32[3]{0:T(128)} %pad_add_fusion.pos, bf16[6,3,2,64,256]{4,3,2,1,0:T(8,128)(2,1)} %copy-done, bf16[6,3,2,64,256]{4,3,2,1,0:T(8,128)(2,1)} %copy-done.1, bf16[2,3,2,64,256]{4,3,2,1,0:T(8,128)(2,1)} %collective-permute-done.1.refs_2_, ...), custom_call_target="tpu_custom_call" | custom-call | flops 1207959552 | bytes 7077888 | tf_op jit(solution)/shard_map/pallas_call | solution.py:64
  105.2 4.3 %collective-permute-done.25.refs_10_ = bf16[4,3,64,256]{3,2,1,0:T(8,128)(2,1)} collective-permute-done((bf16[4,3,64,256]{3,2,1,0:T(8,128)(2,1)S(1)}, bf16[4,3,64,256]{3,2,1,0:T(8,128)(2,1)}, u32[]{:S(2)}, u32[]{:S(2)}) %collective-permute-start.25) | collective-permute-done | bytes 393248 | tf_op jit(solution)/shard_map/ppermute | solution.py:20
  110.2 5.2 %shard_map.61 = (f32[384,256]{1,0:T(8,128)}, f32[384,256]{1,0:T(8,128)}) custom-call(s32[3]{0:T(128)} %pad_add_fusion.pos, bf16[6,3,2,64,256]{4,3,2,1,0:T(8,128)(2,1)} %copy-done, bf16[6,3,2,64,256]{4,3,2,1,0:T(8,128)(2,1)} %copy-done.1, bf16[2,3,2,64,256]{4,3,2,1,0:T(8,128)(2,1)} %collective-permute-done.1.refs_2_, ...), custom_call_target="tpu_custom_call" | custom-call | flops 1207959552 | bytes 7077888 | tf_op jit(solution)/shard_map/pallas_call | solution.py:64
  115.4 3.6 %collective-permute-start.27 = (f32[384,256]{1,0:T(8,128)}, f32[384,256]{1,0:T(8,128)S(1)}, u32[]{:S(2)}, u32[]{:S(2)}) collective-permute-start(f32[384,256]{1,0:T(8,128)} %get-tuple-element.13), channel_id=1, source_target_pairs={{0,4},{1,5},{2,6},{3,7},{4,0},{5,1},{6,2},{7,3},{8,12},{9,13},{10,... | collective-permute-start | bytes 1179656 | tf_op jit(solution)/shard_map/ppermute | solution.py:16
  119.0 10.0 %collective-permute-done.20 = f32[384,256]{1,0:T(8,128)} collective-permute-done((f32[384,256]{1,0:T(8,128)}, f32[384,256]{1,0:T(8,128)}, u32[]{:S(2)}, u32[]{:S(2)}) %collective-permute-start.20) | collective-permute-done | bytes 393248 | tf_op jit(solution)/shard_map/ppermute | solution.py:16
  131.3 3.6 %all-to-all-start.2 = ((f32[4,128,256]{2,1,0:T(8,128)}), f32[4,128,256]{2,1,0:T(8,128)S(1)}, u32[]{:S(2)}, u32[]{:S(2)}) async-start(f32[4,128,256]{2,1,0:T(8,128)} %convolution_bitcast_fusion.1), calls=%async_computation.2 | async-start | bytes 1048576 | tf_op jit(solution)/shard_map/all_to_all | solution.py:101
  141.4 3.5 %all-to-all-start = ((f32[4,128,256]{2,1,0:T(8,128)}), f32[4,128,256]{2,1,0:T(8,128)S(1)}, u32[]{:S(2)}, u32[]{:S(2)}) async-start(f32[4,128,256]{2,1,0:T(8,128)} %convolution_bitcast_fusion.2), calls=%async_computation | async-start | bytes 1048576 | tf_op jit(solution)/shard_map/all_to_all | solution.py:101
  146.2 6.6 %all-to-all-done = f32[4,128,256]{2,1,0:T(8,128)S(1)} async-done(((f32[4,128,256]{2,1,0:T(8,128)}), f32[4,128,256]{2,1,0:T(8,128)S(1)}, u32[]{:S(2)}, u32[]{:S(2)}) %all-to-all-start) | async-done | bytes 524320 | tf_op jit(solution)/shard_map/all_to_all | solution.py:101
  152.8 3.5 %all-to-all-start.4 = ((f32[4,128,256]{2,1,0:T(8,128)}), f32[4,128,256]{2,1,0:T(8,128)S(1)}, u32[]{:S(2)}, u32[]{:S(2)}) async-start(f32[4,128,256]{2,1,0:T(8,128)} %convolution_bitcast_fusion), calls=%async_computation.4 | async-start | bytes 1048576 | tf_op jit(solution)/shard_map/all_to_all | solution.py:101
  158.1 5.3 %all-to-all-done.4 = f32[4,128,256]{2,1,0:T(8,128)S(1)} async-done(((f32[4,128,256]{2,1,0:T(8,128)}), f32[4,128,256]{2,1,0:T(8,128)S(1)}, u32[]{:S(2)}, u32[]{:S(2)}) %all-to-all-start.4) | async-done | bytes 524320 | tf_op jit(solution)/shard_map/all_to_all | solution.py:101
  163.4 4.0 %all-to-all-start.3 = ((f32[8,16,256]{2,1,0:T(8,128)}), f32[8,16,256]{2,1,0:T(8,128)S(1)}, u32[]{:S(2)}, u32[]{:S(2)}) async-start(f32[8,16,256]{2,1,0:T(8,128)} %bitcast.66), calls=%async_computation.3 | async-start | bytes 262144 | tf_op jit(solution)/shard_map/all_to_all | solution.py:103
  169.0 5.1 %all-to-all-done.3 = f32[8,16,256]{2,1,0:T(8,128)S(1)} async-done(((f32[8,16,256]{2,1,0:T(8,128)}), f32[8,16,256]{2,1,0:T(8,128)S(1)}, u32[]{:S(2)}, u32[]{:S(2)}) %all-to-all-start.3) | async-done | bytes 131104 | tf_op jit(solution)/shard_map/all_to_all | solution.py:103
  174.1 3.4 %all-to-all-start.1 = ((f32[8,16,256]{2,1,0:T(8,128)}), f32[8,16,256]{2,1,0:T(8,128)S(1)}, u32[]{:S(2)}, u32[]{:S(2)}) async-start(f32[8,16,256]{2,1,0:T(8,128)} %bitcast.57), calls=%async_computation.1 | async-start | bytes 262144 | tf_op jit(solution)/shard_map/all_to_all | solution.py:103
  178.2 5.9 %all-to-all-done.1 = f32[8,16,256]{2,1,0:T(8,128)S(1)} async-done(((f32[8,16,256]{2,1,0:T(8,128)}), f32[8,16,256]{2,1,0:T(8,128)S(1)}, u32[]{:S(2)}, u32[]{:S(2)}) %all-to-all-start.1) | async-done | bytes 131104 | tf_op jit(solution)/shard_map/all_to_all | solution.py:103
  184.2 3.4 %all-to-all-start.5 = ((f32[8,16,256]{2,1,0:T(8,128)}), f32[8,16,256]{2,1,0:T(8,128)S(1)}, u32[]{:S(2)}, u32[]{:S(2)}) async-start(f32[8,16,256]{2,1,0:T(8,128)} %bitcast.75), calls=%async_computation.5 | async-start | bytes 262144 | tf_op jit(solution)/shard_map/all_to_all | solution.py:103
  188.7 5.6 %all-to-all-done.5 = f32[8,16,256]{2,1,0:T(8,128)S(1)} async-done(((f32[8,16,256]{2,1,0:T(8,128)}), f32[8,16,256]{2,1,0:T(8,128)S(1)}, u32[]{:S(2)}, u32[]{:S(2)}) %all-to-all-start.5) | async-done | bytes 131104 | tf_op jit(solution)/shard_map/all_to_all | solution.py:103
  (144 shorter events, 64.6 us)
Async XLA Ops:
  3.5 15.8 %collective-permute-start.7 = (bf16[3,6,32,512]{3,2,1,0:T(8,128)(2,1)}, bf16[3,6,32,512]{3,2,1,0:T(8,128)(2,1)}, u32[]{:S(2)}, u32[]{:S(2)}) collective-permute-start(bf16[3,6,32,512]{3,2,1,0:T(8,128)(2,1)} %bitcast_multiply_fusion), channel_id=1, source_target_pairs={{0,1},{1,0},{2,3},{3,2},{4,5},{5,4},{6,7},{7,6},{8,9},{9,8},{10,11... | collective-permute-start | bytes 1769480 | tf_op jit(solution)/shard_map/ppermute | solution.py:16
  6.5 12.8 %collective-permute-start.1 = (bf16[2,3,2,64,256]{4,3,2,1,0:T(8,128)(2,1)}, bf16[2,3,2,64,256]{4,3,2,1,0:T(8,128)(2,1)}, u32[]{:S(2)}, u32[]{:S(2)}) collective-permute-start(bf16[2,3,2,64,256]{4,3,2,1,0:T(8,128)(2,1)} %get-tuple-element.24), channel_id=1, source_target_pairs={{0,2},{1,3},{2,0},{3,1},{4,6},{5,7},{6,4},{7,5},{8,10},{9,11},{10,... | collective-permute-start | bytes 1179656 | tf_op jit(solution)/shard_map/ppermute | solution.py:16
  9.2 54.6 %collective-permute-start = (bf16[6,3,2,64,256]{4,3,2,1,0:T(8,128)(2,1)S(1)}, bf16[6,3,2,64,256]{4,3,2,1,0:T(8,128)(2,1)S(1)}, u32[]{:S(2)}, u32[]{:S(2)}) collective-permute-start(bf16[6,3,2,64,256]{4,3,2,1,0:T(8,128)(2,1)S(1)} %dynamic-slice_bitcast_fusion.refs_0_), channel_id=1, source_target_pairs={{0,1},{1,0},{2,3},{3,2},{4,5},{5,4},{6,7},{7,6},{8,9},{9,8},{10,11... | collective-permute-start | bytes 3538952 | tf_op jit(solution)/shard_map/ppermute | solution.py:16
  9.5 20.4 %collective-permute-start.2 = (bf16[2,3,2,64,256]{4,3,2,1,0:T(8,128)(2,1)}, bf16[2,3,2,64,256]{4,3,2,1,0:T(8,128)(2,1)}, u32[]{:S(2)}, u32[]{:S(2)}) collective-permute-start(bf16[2,3,2,64,256]{4,3,2,1,0:T(8,128)(2,1)} %get-tuple-element.23), channel_id=1, source_target_pairs={{0,2},{1,3},{2,0},{3,1},{4,6},{5,7},{6,4},{7,5},{8,10},{9,11},{10,... | collective-permute-start | bytes 1179656 | tf_op jit(solution)/shard_map/ppermute | solution.py:16
  9.8 30.5 %collective-permute-start.3 = (bf16[2,3,2,64,256]{4,3,2,1,0:T(8,128)(2,1)}, bf16[2,3,2,64,256]{4,3,2,1,0:T(8,128)(2,1)}, u32[]{:S(2)}, u32[]{:S(2)}) collective-permute-start(bf16[2,3,2,64,256]{4,3,2,1,0:T(8,128)(2,1)} %get-tuple-element.22), channel_id=1, source_target_pairs={{0,2},{1,3},{2,0},{3,1},{4,6},{5,7},{6,4},{7,5},{8,10},{9,11},{10,... | collective-permute-start | bytes 1179656 | tf_op jit(solution)/shard_map/ppermute | solution.py:16
  19.4 29.2 %collective-permute-start.4 = (bf16[2,3,2,64,256]{4,3,2,1,0:T(8,128)(2,1)}, bf16[2,3,2,64,256]{4,3,2,1,0:T(8,128)(2,1)S(1)}, u32[]{:S(2)}, u32[]{:S(2)}) collective-permute-start(bf16[2,3,2,64,256]{4,3,2,1,0:T(8,128)(2,1)} %collective-permute-done.1.refs_2_), channel_id=1, source_target_pairs={{0,1},{1,0},{2,3},{3,2},{4,5},{5,4},{6,7},{7,6},{8,9},{9,8},{10,11... | collective-permute-start | bytes 1179656 | tf_op jit(solution)/shard_map/ppermute | solution.py:16
  20.9 19.3 %collective-permute-start.15 = (bf16[3,64,256]{2,1,0:T(8,128)(2,1)S(1)}, bf16[3,64,256]{2,1,0:T(8,128)(2,1)S(1)}, u32[]{:S(2)}, u32[]{:S(2)}) collective-permute-start(bf16[3,64,256]{2,1,0:T(8,128)(2,1)S(1)} %get-tuple-element.46), channel_id=1, source_target_pairs={{0,4},{1,5},{2,6},{3,7},{4,0},{5,1},{6,2},{7,3},{8,12},{9,13},{10,... | collective-permute-start | bytes 294920 | tf_op jit(solution)/shard_map/ppermute | solution.py:16
  40.3 16.9 %collective-permute-start.5 = (bf16[2,3,2,64,256]{4,3,2,1,0:T(8,128)(2,1)}, bf16[2,3,2,64,256]{4,3,2,1,0:T(8,128)(2,1)S(1)}, u32[]{:S(2)}, u32[]{:S(2)}) collective-permute-start(bf16[2,3,2,64,256]{4,3,2,1,0:T(8,128)(2,1)} %collective-permute-done.2.refs_3_), channel_id=1, source_target_pairs={{0,1},{1,0},{2,3},{3,2},{4,5},{5,4},{6,7},{7,6},{8,9},{9,8},{10,11... | collective-permute-start | bytes 1179656 | tf_op jit(solution)/shard_map/ppermute | solution.py:16
  40.3 18.5 %collective-permute-start.6 = (bf16[2,3,2,64,256]{4,3,2,1,0:T(8,128)(2,1)}, bf16[2,3,2,64,256]{4,3,2,1,0:T(8,128)(2,1)S(1)}, u32[]{:S(2)}, u32[]{:S(2)}) collective-permute-start(bf16[2,3,2,64,256]{4,3,2,1,0:T(8,128)(2,1)} %collective-permute-done.3.refs_4_), channel_id=1, source_target_pairs={{0,1},{1,0},{2,3},{3,2},{4,5},{5,4},{6,7},{7,6},{8,9},{9,8},{10,11... | collective-permute-start | bytes 1179656 | tf_op jit(solution)/shard_map/ppermute | solution.py:16
  57.1 12.3 %collective-permute-start.17 = (bf16[4,3,64,256]{3,2,1,0:T(8,128)(2,1)}, bf16[4,3,64,256]{3,2,1,0:T(8,128)(2,1)}, u32[]{:S(2)}, u32[]{:S(2)}) collective-permute-start(bf16[4,3,64,256]{3,2,1,0:T(8,128)(2,1)} %bitcast.31.refs_8_), channel_id=1, source_target_pairs={{0,8},{8,0},{16,24},{24,16},{1,9},{9,1},{17,25},{25,17},{2,10},{10... | collective-permute-start | bytes 1179656 | tf_op jit(solution)/shard_map/ppermute | solution.py:20
  58.8 20.3 %collective-permute-start.18 = (bf16[4,3,64,256]{3,2,1,0:T(8,128)(2,1)}, bf16[4,3,64,256]{3,2,1,0:T(8,128)(2,1)}, u32[]{:S(2)}, u32[]{:S(2)}) collective-permute-start(bf16[4,3,64,256]{3,2,1,0:T(8,128)(2,1)} %bitcast.31.refs_8_), channel_id=1, source_target_pairs={{0,16},{8,24},{16,0},{24,8},{1,17},{9,25},{17,1},{25,9},{2,18},{10... | collective-permute-start | bytes 1179656 | tf_op jit(solution)/shard_map/ppermute | solution.py:20
  60.3 18.8 %collective-permute-start.19 = (bf16[4,3,64,256]{3,2,1,0:T(8,128)(2,1)}, bf16[4,3,64,256]{3,2,1,0:T(8,128)(2,1)}, u32[]{:S(2)}, u32[]{:S(2)}) collective-permute-start(bf16[4,3,64,256]{3,2,1,0:T(8,128)(2,1)} %bitcast.31.refs_8_), channel_id=1, source_target_pairs={{0,24},{8,16},{16,8},{24,0},{1,25},{9,17},{17,9},{25,1},{2,26},{10... | collective-permute-start | bytes 1179656 | tf_op jit(solution)/shard_map/ppermute | solution.py:20
  63.3 23.0 %collective-permute-start.10 = (bf16[4,3,64,256]{3,2,1,0:T(8,128)(2,1)}, bf16[4,3,64,256]{3,2,1,0:T(8,128)(2,1)}, u32[]{:S(2)}, u32[]{:S(2)}) collective-permute-start(bf16[4,3,64,256]{3,2,1,0:T(8,128)(2,1)} %bitcast.18.refs_8_), channel_id=1, source_target_pairs={{0,8},{8,0},{16,24},{24,16},{1,9},{9,1},{17,25},{25,17},{2,10},{10... | collective-permute-start | bytes 1179656 | tf_op jit(solution)/shard_map/ppermute | solution.py:20
  64.0 31.8 %collective-permute-start.11 = (bf16[4,3,64,256]{3,2,1,0:T(8,128)(2,1)}, bf16[4,3,64,256]{3,2,1,0:T(8,128)(2,1)S(1)}, u32[]{:S(2)}, u32[]{:S(2)}) collective-permute-start(bf16[4,3,64,256]{3,2,1,0:T(8,128)(2,1)} %bitcast.18.refs_8_), channel_id=1, source_target_pairs={{0,16},{8,24},{16,0},{24,8},{1,17},{9,25},{17,1},{25,9},{2,18},{10... | collective-permute-start | bytes 1179656 | tf_op jit(solution)/shard_map/ppermute | solution.py:20
  69.4 30.2 %collective-permute-start.12 = (bf16[4,3,64,256]{3,2,1,0:T(8,128)(2,1)}, bf16[4,3,64,256]{3,2,1,0:T(8,128)(2,1)}, u32[]{:S(2)}, u32[]{:S(2)}) collective-permute-start(bf16[4,3,64,256]{3,2,1,0:T(8,128)(2,1)} %bitcast.18.refs_8_), channel_id=1, source_target_pairs={{0,24},{8,16},{16,8},{24,0},{1,25},{9,17},{17,9},{25,1},{2,26},{10... | collective-permute-start | bytes 1179656 | tf_op jit(solution)/shard_map/ppermute | solution.py:20
  79.1 26.1 %collective-permute-start.24 = (bf16[4,3,64,256]{3,2,1,0:T(8,128)(2,1)S(1)}, bf16[4,3,64,256]{3,2,1,0:T(8,128)(2,1)}, u32[]{:S(2)}, u32[]{:S(2)}) collective-permute-start(bf16[4,3,64,256]{3,2,1,0:T(8,128)(2,1)S(1)} %bitcast.149), channel_id=1, source_target_pairs={{0,8},{8,0},{16,24},{24,16},{1,9},{9,1},{17,25},{25,17},{2,10},{10... | collective-permute-start | bytes 1179656 | tf_op jit(solution)/shard_map/ppermute | solution.py:20
  79.1 30.4 %collective-permute-start.25 = (bf16[4,3,64,256]{3,2,1,0:T(8,128)(2,1)S(1)}, bf16[4,3,64,256]{3,2,1,0:T(8,128)(2,1)}, u32[]{:S(2)}, u32[]{:S(2)}) collective-permute-start(bf16[4,3,64,256]{3,2,1,0:T(8,128)(2,1)S(1)} %bitcast.150), channel_id=1, source_target_pairs={{0,16},{8,24},{16,0},{24,8},{1,17},{9,25},{17,1},{25,9},{2,18},{10... | collective-permute-start | bytes 1179656 | tf_op jit(solution)/shard_map/ppermute | solution.py:20
  86.3 23.1 %collective-permute-start.26 = (bf16[4,3,64,256]{3,2,1,0:T(8,128)(2,1)S(1)}, bf16[4,3,64,256]{3,2,1,0:T(8,128)(2,1)S(1)}, u32[]{:S(2)}, u32[]{:S(2)}) collective-permute-start(bf16[4,3,64,256]{3,2,1,0:T(8,128)(2,1)S(1)} %bitcast.151), channel_id=1, source_target_pairs={{0,24},{8,16},{16,8},{24,0},{1,25},{9,17},{17,9},{25,1},{2,26},{10... | collective-permute-start | bytes 1179656 | tf_op jit(solution)/shard_map/ppermute | solution.py:20
  95.8 33.2 %collective-permute-start.20 = (f32[384,256]{1,0:T(8,128)}, f32[384,256]{1,0:T(8,128)}, u32[]{:S(2)}, u32[]{:S(2)}) collective-permute-start(f32[384,256]{1,0:T(8,128)} %get-tuple-element.11), channel_id=1, source_target_pairs={{0,4},{1,5},{2,6},{3,7},{4,0},{5,1},{6,2},{7,3},{8,12},{9,13},{10,... | collective-permute-start | bytes 1179656 | tf_op jit(solution)/shard_map/ppermute | solution.py:16
  104.8 32.6 %collective-permute-start.13 = (f32[384,256]{1,0:T(8,128)}, f32[384,256]{1,0:T(8,128)}, u32[]{:S(2)}, u32[]{:S(2)}) collective-permute-start(f32[384,256]{1,0:T(8,128)} %get-tuple-element.9), channel_id=1, source_target_pairs={{0,4},{1,5},{2,6},{3,7},{4,0},{5,1},{6,2},{7,3},{8,12},{9,13},{10,... | collective-permute-start | bytes 1179656 | tf_op jit(solution)/shard_map/ppermute | solution.py:16
  115.4 29.5 %collective-permute-start.27 = (f32[384,256]{1,0:T(8,128)}, f32[384,256]{1,0:T(8,128)S(1)}, u32[]{:S(2)}, u32[]{:S(2)}) collective-permute-start(f32[384,256]{1,0:T(8,128)} %get-tuple-element.13), channel_id=1, source_target_pairs={{0,4},{1,5},{2,6},{3,7},{4,0},{5,1},{6,2},{7,3},{8,12},{9,13},{10,... | collective-permute-start | bytes 1179656 | tf_op jit(solution)/shard_map/ppermute | solution.py:16
  135.7 20.8 %collective-permute-start.21 = (bf16[6,32,256]{2,1,0:T(8,128)(2,1)}, bf16[6,32,256]{2,1,0:T(8,128)(2,1)}, u32[]{:S(2)}, u32[]{:S(2)}) collective-permute-start(bf16[6,32,256]{2,1,0:T(8,128)(2,1)} %dynamic-slice_bitcast_fusion.7), channel_id=1, source_target_pairs={{0,1},{1,0},{2,3},{3,2},{4,5},{5,4},{6,7},{7,6},{8,9},{9,8},{10,11... | collective-permute-start | bytes 294920 | tf_op jit(solution)/shard_map/ppermute | solution.py:16
  139.2 28.1 %collective-permute-start.14 = (bf16[6,32,256]{2,1,0:T(8,128)(2,1)}, bf16[6,32,256]{2,1,0:T(8,128)(2,1)}, u32[]{:S(2)}, u32[]{:S(2)}) collective-permute-start(bf16[6,32,256]{2,1,0:T(8,128)(2,1)} %dynamic-slice_bitcast_fusion.10), channel_id=1, source_target_pairs={{0,1},{1,0},{2,3},{3,2},{4,5},{5,4},{6,7},{7,6},{8,9},{9,8},{10,11... | collective-permute-start | bytes 294920 | tf_op jit(solution)/shard_map/ppermute | solution.py:16
  156.4 21.1 %collective-permute-start.28 = (bf16[6,32,256]{2,1,0:T(8,128)(2,1)S(1)}, bf16[6,32,256]{2,1,0:T(8,128)(2,1)S(1)}, u32[]{:S(2)}, u32[]{:S(2)}) collective-permute-start(bf16[6,32,256]{2,1,0:T(8,128)(2,1)S(1)} %dynamic-slice_bitcast_fusion.4), channel_id=1, source_target_pairs={{0,1},{1,0},{2,3},{3,2},{4,5},{5,4},{6,7},{7,6},{8,9},{9,8},{10,11... | collective-permute-start | bytes 294920 | tf_op jit(solution)/shard_map/ppermute | solution.py:16
  (29 other events, 246.5 us)
